TPU v7x, 32 devices: a whole 2x2x4 slice. The times are simulated.
32 devices in a mesh: grp: 4 (over y, core), dev: 8 (over z, x).
Axes of the slice: x: 2, y: 2, z: 4, core: 2. Of those that a mesh axis runs over, the one named last changes fastest.
Arguments:
- train_grads: bfloat16 [4096, 1024], P(('grp', 'dev')), may hold values from -192 to 192, as said below
- queries: bfloat16 [512, 1024], P('grp'), may hold values from -6 to 6
Outputs:
- scores: bfloat16 [4096, 512], P(('grp', 'dev'))
Inputs may be any that keep to these rules, and one draw needn't show every extreme that they name: `train_grads`: Real-valued projected gradients whose columns and rows differ in scale.
All inputs are finite; a program needn't handle non-finite values. Where the computation divides by a largest or mean magnitude, that divisor is 1e-20 or more.
Results may differ from a plain program's by a relative error of at most 0.001.
The roundings to bfloat16 on the way count: a program that leaves them out, or rounds other values in their place, can miss the bound.
Values may be sent and summed in bfloat16 or wider, within the bound.
No kernel may reach another device: no remote copies, remote signals or barrier semaphores. Data moves between devices by JAX's collectives and lax.ppermute only.
A program may use at most 64 MiB of HBM per device.

v0:
```python
import jax
import jax.numpy as jnp
from jax import lax
from jax.sharding import PartitionSpec as P

ITERS = 8
damping_ratio = 0.1


def local_solve(gram, own, total, width):
    normed = gram / total
    damp = damping_ratio * jnp.trace(gram) / (total * width)
    bound = jnp.max(jnp.sum(jnp.abs(normed), axis=1)) + damp
    step = 1.0 / bound
    oper = normed + damp * jnp.eye(width, dtype=jnp.float32)
    state = step * own
    for index in range(ITERS):
        state = state + step * (own - jnp.dot(state, oper, precision=lax.Precision.HIGHEST))
    return state.astype(jnp.bfloat16)


def body(train_grads, queries):
    rows, width = train_grads.shape
    ndevice = lax.axis_size("dev")
    total = rows * ndevice * lax.axis_size("grp")
    qvals = queries.astype(jnp.float32)
    qrows = qvals.shape[0] // ndevice
    qstart = lax.axis_index("dev") * qrows
    own = lax.dynamic_slice_in_dim(qvals, qstart, qrows, 0)
    gram = lax.psum(
        lax.dot_general(
            train_grads, train_grads, (((0,), (0,)), ((), ())), preferred_element_type=jnp.float32
        ),
        ("grp", "dev"),
    )
    mine = local_solve(gram, own, total, width)
    prepared = lax.all_gather(mine, "dev", axis=0, tiled=True)
    return lax.dot_general(
        train_grads,
        lax.all_gather(prepared, "grp", axis=0, tiled=True),
        (((1,), (1,)), ((), ())),
        preferred_element_type=jnp.float32,
    ).astype(jnp.bfloat16)


def solution(mesh):
    return jax.shard_map(
        body,
        mesh=mesh,
        in_specs=(P(("grp", "dev"), None), P("grp", None)),
        out_specs=P(("grp", "dev"), None),
        check_vma=False,
    )
```

profile of v0, /device:TPU:0, one launch (start us, length us, event | category | flops | bytes accessed | tf_op | source)
XLA Modules:
  0.0 242.2 jit_solution(13720680544935687470)
XLA Ops:
  6.5 0.0 copy-start
  6.5 0.0 all-reduce.2.cloned.1.call-start
  6.5 0.9 copy-done
  7.5 2.7 %fusion.21 = f32[1024,1024]{1,0:T(8,128)} fusion(bf16[128,1024]{1,0:T(8,128)(2,1)S(1)} %copy-done), kind=kOutput, calls=%fused_computation.35 | convolution fusion | flops 268435456 | bytes 4456448 | tf_op jit(solution)/shard_map/dot_general | solution.py:31
  10.2 0.0 copy-start.2
  10.2 0.0 all-reduce.2.cloned.1.call-update
  10.2 0.0 all-gather.2.cloned.1.call-start
  10.3 147.6 %all-reduce.2.cloned.1.call-done = f32[1024,1024]{1,0:T(8,128)} async-done(((f32[1024,1024]{1,0:T(8,128)}), f32[1024,1024]{1,0:T(8,128)}) %all-reduce.2.cloned.1.call-update) | async-done | bytes 4194320 | tf_op jit(solution)/shard_map/psum | solution.py:30
  157.9 3.3 %select_reduce_fusion = (f32[]{:T(128)}, f32[1024]{0:T(1024)S(1)}) fusion(f32[1024,1024]{1,0:T(8,128)} %all-reduce.2.cloned.1.call-done), kind=kLoop, calls=%fused_computation.1 | loop fusion | flops 6290431 | bytes 4198404 | tf_op jit(solution)/shard_map/jit(trace)/reduce_sum | solution.py:12
  161.9 0.6 reduce_max.9
  163.2 0.0 copy-done.2
  163.2 0.0 copy-start.1
  163.2 4.6 %fusion.2 = f32[16,1024]{1,0:T(8,128)S(1)} fusion(f32[]{:T(128)S(6)} %div.15, bf16[128,1024]{1,0:T(8,128)(2,1)S(1)} %copy-done.2, s32[]{:T(128)S(6)} %select_n.9, f32[1024,1024]{1,0:T(8,128)} %all-reduce.2.cloned.1.call-done, f32[]{:T(128)S(6)} %div.14), kind=kOutput, calls=%fused_computation.15 | convolution fusion | flops 205635584 | bytes 4327936 | tf_op jit(solution)/shard_map/dot_general | solution.py:18
  167.8 0.0 copy-done.1
  167.8 2.3 fusion.4
  170.1 2.3 fusion.6
  172.3 2.3 fusion.8
  174.6 2.3 fusion.10
  176.8 2.4 %fusion.12 = f32[16,1024]{1,0:T(8,128)S(1)} fusion(f32[16,1024]{1,0:T(8,128)S(1)} %fusion.10, f32[]{:T(128)S(6)} %div.15, bf16[128,1024]{1,0:T(8,128)(2,1)S(1)} %copy-done.2, s32[]{:T(128)S(6)} %select_n.9, f32[1024,1024]{1,0:T(8,128)S(1)} %copy-done.1, f32[]{:T(128)S(6)} %div.14), kind=kOutput, calls=%fused_computation.25 | convolution fusion | flops 205586432 | bytes 4423692 | tf_op jit(solution)/shard_map/dot_general | solution.py:18
  179.3 2.3 fusion.14
  181.5 2.3 fusion.17
  183.8 32.8 %all_gather.6 = bf16[128,1024]{1,0:T(8,128)(2,1)} all-gather(bf16[16,1024]{1,0:T(8,128)(2,1)S(1)} %fusion.17), channel_id=1, replica_groups=mesh['grp'=4,'dev'=8] {'dev'}, dimensions={0}, use_global_device_ids=true | all-gather | bytes 294912 | tf_op jit(solution)/shard_map/all_gather | solution.py:37
  216.6 0.0 all-gather.2.cloned.1.call-update
  216.7 16.3 %all-gather.2.cloned.1.call-done = bf16[512,1024]{1,0:T(8,128)(2,1)} async-done(((bf16[128,1024]{1,0:T(8,128)(2,1)}), bf16[512,1024]{1,0:T(8,128)(2,1)}) %all-gather.2.cloned.1.call-update) | async-done | bytes 1048592 | tf_op jit(solution)/shard_map/all_gather | solution.py:40
  233.0 1.7 fusion
  234.6 0.8 copy.3
Async XLA Ops:
  6.5 1.0 copy-start
  6.5 151.4 %all-reduce.2.cloned.1.call-start = ((), (), s32[]{:S(2)}) async-start(), calls=%async_computation | async-start | bytes 8388608 | tf_op jit(solution)/shard_map/psum | solution.py:30
  10.2 153.0 %copy-start.2 = (bf16[128,1024]{1,0:T(8,128)(2,1)S(1)}, bf16[128,1024]{1,0:T(8,128)(2,1)}, u32[]{:S(2)}) copy-start(bf16[128,1024]{1,0:T(8,128)(2,1)} %param.3) | copy-start | bytes 786436
  10.2 222.8 %all-gather.2.cloned.1.call-start = ((), (), s32[]{:S(2)}) async-start(), calls=%async_computation.1 | async-start | bytes 1310720 | tf_op jit(solution)/shard_map/all_gather | solution.py:40
  163.2 4.6 %copy-start.1 = (f32[1024,1024]{1,0:T(8,128)S(1)}, f32[1024,1024]{1,0:T(8,128)}, u32[]{:S(2)}) copy-start(f32[1024,1024]{1,0:T(8,128)} %all-reduce.2.cloned.1.call-done) | copy-start | bytes 12582916
Sparse Core Ops, SparseCore 0:
  12.9 144.9 all-reduce.1
  216.8 16.1 all-gather.1
where the time goes:
time: 242 us
  waiting for transfers between devices  164 us (68%)
  blocking collectives  32.8 us (14%)
  matrix products  24.9 us (10%)
  between operations  14.8 us (6%)
  other arithmetic  3.94 us (2%)
    psum x1, waiting for transfers between devices, body(): lax.psum(lax.dot_general(train_grads, train_grads, (((0,), (0,)), ((), ()...  148 us
    all_gather x1, blocking collectives, body(): prepared = lax.all_gather(mine, 'dev', axis=0, tiled=True)  32.8 us
    dot_general x8, matrix products, local_solve(): jnp.dot(state, oper, precision=lax.Precision.HIGHEST)  20.5 us
    all_gather x1, waiting for transfers between devices, body(): lax.all_gather(prepared, 'grp', axis=0, tiled=True)  16.3 us
  transfers between devices with their start and end apart: 2, of which 2 were waited for; matrix products, arithmetic and copies ran while one was open for 0% of the time, Pallas kernels for 0%

commit v1 on v0

--- a/solution.py
+++ b/solution.py
@@ -5,6 +5,30 @@
 
 ITERS = 8
 damping_ratio = 0.1
+
+
+def copies_pass(incoming_x, dim_at):
+    incoming_x = jnp.moveaxis(incoming_x, 0, dim_at)
+    x_now = incoming_x.shape
+    return incoming_x.reshape(
+        *x_now[:dim_at], x_now[dim_at] * x_now[dim_at + 1], *x_now[dim_at + 2 :]
+    )
+
+
+def sector_edit(vec, a_name):
+    y_new = lax.axis_size(a_name)
+    w1 = lax.axis_index(a_name)
+    val2, piece_out = (y_new, w1)
+    known, passed = (vec[None], 1)
+    while passed < val2:
+        t1 = list(map(lambda tick: (tick, tick ^ passed), range(val2)))
+        f_next = lax.ppermute(known, a_name, t1)
+        mid_arr = piece_out & passed == 0
+        known = jnp.concatenate(
+            [jnp.where(mid_arr, known, f_next), jnp.where(mid_arr, f_next, known)]
+        )
+        passed *= 2
+    return known
 
 
 def local_solve(gram, own, total, width):
@@ -34,7 +58,8 @@
         ("grp", "dev"),
     )
     mine = local_solve(gram, own, total, width)
-    prepared = lax.all_gather(mine, "dev", axis=0, tiled=True)
+    kept_arr = sector_edit(mine, "dev")
+    prepared = copies_pass(kept_arr, 0)
     return lax.dot_general(
         train_grads,
         lax.all_gather(prepared, "grp", axis=0, tiled=True),

time: 242 us -> 226 us (0.934)
  blocking collectives: 32.8 us -> 0 us
  waiting for transfers between devices: 164 us -> 177 us
  starting transfers between devices: 0.04 us -> 3.4 us
    all_gather x1 -> x0, blocking collectives: 32.8 us -> none  [body(): prepared = lax.all_gather(mine, 'dev', axis=0, tiled=True)]
    ppermute x0 -> x3, waiting for transfers between devices: none -> 13.2 us  [sector_edit(): f_next = lax.ppermute(known, a_name, t1)]
    ppermute x0 -> x3, starting transfers between devices: none -> 3.36 us  [sector_edit(): f_next = lax.ppermute(known, a_name, t1)]
  transfers between devices with their start and end apart: 2 -> 5, of which waited for: 2 -> 5; matrix products, arithmetic and copies ran while one was open for 0% -> 0% of each run, Pallas kernels for 0% -> 0%
where the time goes in v1:
time: 226 us
  waiting for transfers between devices  177 us (78%)
  matrix products  24.9 us (11%)
  between operations  14.9 us (7%)
  other arithmetic  4.73 us (2%)
  starting transfers between devices  3.4 us (2%)
    psum x1, waiting for transfers between devices, body(): lax.psum(lax.dot_general(train_grads, train_grads, (((0,), (0,)), ((), ()...  148 us
    dot_general x8, matrix products, local_solve(): jnp.dot(state, oper, precision=lax.Precision.HIGHEST)  20.5 us
    all_gather x1, waiting for transfers between devices, body(): lax.all_gather(prepared, 'grp', axis=0, tiled=True)  15.4 us
    ppermute x3, waiting for transfers between devices, sector_edit(): f_next = lax.ppermute(known, a_name, t1)  13.2 us
  transfers between devices with their start and end apart: 5, of which 5 were waited for; matrix products, arithmetic and copies ran while one was open for 0% of the time, Pallas kernels for 0%

profile of v1, /device:TPU:0, one launch (start us, length us, event | category | flops | bytes accessed | tf_op | source)
XLA Modules:
  0.0 226.1 jit_solution(14214115463304786477)
XLA Ops:
  6.5 0.0 copy-start
  6.5 0.0 all-reduce.2.cloned.1.call-start
  6.5 0.9 copy-done
  7.5 2.7 %fusion.22 = f32[1024,1024]{1,0:T(8,128)} fusion(bf16[128,1024]{1,0:T(8,128)(2,1)S(1)} %copy-done), kind=kOutput, calls=%fused_computation.45 | convolution fusion | flops 268435456 | bytes 4456448 | tf_op jit(solution)/shard_map/dot_general | solution.py:55
  10.2 0.0 copy-start.2
  10.2 0.0 all-reduce.2.cloned.1.call-update
  10.2 0.0 all-gather.2.cloned.1.call-start
  10.3 147.9 %all-reduce.2.cloned.1.call-done = f32[1024,1024]{1,0:T(8,128)} async-done(((f32[1024,1024]{1,0:T(8,128)}), f32[1024,1024]{1,0:T(8,128)}) %all-reduce.2.cloned.1.call-update) | async-done | bytes 4194320 | tf_op jit(solution)/shard_map/psum | solution.py:54
  158.2 3.3 %select_reduce_fusion = (f32[]{:T(128)}, f32[1024]{0:T(1024)S(1)}) fusion(f32[1024,1024]{1,0:T(8,128)} %all-reduce.2.cloned.1.call-done), kind=kLoop, calls=%fused_computation.1 | loop fusion | flops 6290431 | bytes 4198404 | tf_op jit(solution)/shard_map/jit(trace)/reduce_sum | solution.py:36
  162.1 0.6 reduce_max.9
  163.4 0.0 copy-done.2
  163.4 0.0 copy-start.1
  163.5 4.6 %fusion.2 = f32[16,1024]{1,0:T(8,128)S(1)} fusion(f32[]{:T(128)S(6)} %div.15, bf16[128,1024]{1,0:T(8,128)(2,1)S(1)} %copy-done.2, s32[]{:T(128)S(6)} %select_n.48, f32[1024,1024]{1,0:T(8,128)} %all-reduce.2.cloned.1.call-done, f32[]{:T(128)S(6)} %div.14), kind=kOutput, calls=%fused_computation.15 | convolution fusion | flops 205635584 | bytes 4327936 | tf_op jit(solution)/shard_map/dot_general | solution.py:42
  168.1 0.0 copy-done.1
  168.1 2.3 fusion.4
  170.3 2.3 fusion.6
  172.6 2.3 fusion.8
  174.8 2.3 fusion.10
  177.1 2.4 %fusion.12 = f32[16,1024]{1,0:T(8,128)S(1)} fusion(f32[16,1024]{1,0:T(8,128)S(1)} %fusion.10, f32[]{:T(128)S(6)} %div.15, bf16[128,1024]{1,0:T(8,128)(2,1)S(1)} %copy-done.2, s32[]{:T(128)S(6)} %select_n.48, f32[1024,1024]{1,0:T(8,128)S(1)} %copy-done.1, f32[]{:T(128)S(6)} %div.14), kind=kOutput, calls=%fused_computation.25 | convolution fusion | flops 205586432 | bytes 4423692 | tf_op jit(solution)/shard_map/dot_general | solution.py:42
  179.5 2.3 fusion.14
  181.8 2.3 fusion.18
  184.1 1.4 collective-permute-start
  185.5 2.6 %collective-permute-done = bf16[1,16,1024]{2,1,0:T(8,128)(2,1)S(1)} collective-permute-done((bf16[1,16,1024]{2,1,0:T(8,128)(2,1)S(1)}, bf16[1,16,1024]{2,1,0:T(8,128)(2,1)S(1)}, u32[]{:S(2)}, u32[]{:S(2)}) %collective-permute-start) | collective-permute-done | bytes 32800 | tf_op jit(solution)/shard_map/ppermute | solution.py:25
  188.1 0.8 collective-permute-start.1
  188.9 4.6 %collective-permute-done.1 = bf16[2,16,1024]{2,1,0:T(8,128)(2,1)S(1)} collective-permute-done((bf16[2,16,1024]{2,1,0:T(8,128)(2,1)S(1)}, bf16[2,16,1024]{2,1,0:T(8,128)(2,1)S(1)}, u32[]{:S(2)}, u32[]{:S(2)}) %collective-permute-start.1) | collective-permute-done | bytes 65568 | tf_op jit(solution)/shard_map/ppermute | solution.py:25
  193.6 1.1 collective-permute-start.2
  194.7 6.0 %collective-permute-done.2 = bf16[4,16,1024]{2,1,0:T(8,128)(2,1)S(1)} collective-permute-done((bf16[4,16,1024]{2,1,0:T(8,128)(2,1)S(1)}, bf16[4,16,1024]{2,1,0:T(8,128)(2,1)S(1)}, u32[]{:S(2)}, u32[]{:S(2)}) %collective-permute-start.2) | collective-permute-done | bytes 131104 | tf_op jit(solution)/shard_map/ppermute | solution.py:25
  200.7 0.7 pad_maximum_fusion
  201.4 0.0 all-gather.2.cloned.1.call-update
  201.5 15.4 %all-gather.2.cloned.1.call-done = bf16[512,1024]{1,0:T(8,128)(2,1)} async-done(((bf16[128,1024]{1,0:T(8,128)(2,1)}), bf16[512,1024]{1,0:T(8,128)(2,1)}) %all-gather.2.cloned.1.call-update) | async-done | bytes 1048592 | tf_op jit(solution)/shard_map/all_gather | solution.py:65
  216.9 1.7 fusion
  218.5 0.8 copy.3
  (5 shorter events, 0.1 us)
Async XLA Ops:
  6.5 1.0 copy-start
  6.5 151.6 %all-reduce.2.cloned.1.call-start = ((), (), s32[]{:S(2)}) async-start(), calls=%async_computation | async-start | bytes 8388608 | tf_op jit(solution)/shard_map/psum | solution.py:54
  10.2 153.3 %copy-start.2 = (bf16[128,1024]{1,0:T(8,128)(2,1)S(1)}, bf16[128,1024]{1,0:T(8,128)(2,1)}, u32[]{:S(2)}) copy-start(bf16[128,1024]{1,0:T(8,128)(2,1)} %param.3) | copy-start | bytes 786436
  10.2 206.7 %all-gather.2.cloned.1.call-start = ((), (), s32[]{:S(2)}) async-start(), calls=%async_computation.1 | async-start | bytes 1310720 | tf_op jit(solution)/shard_map/all_gather | solution.py:65
  163.4 4.6 %copy-start.1 = (f32[1024,1024]{1,0:T(8,128)S(1)}, f32[1024,1024]{1,0:T(8,128)}, u32[]{:S(2)}) copy-start(f32[1024,1024]{1,0:T(8,128)} %all-reduce.2.cloned.1.call-done) | copy-start | bytes 12582916
  184.1 4.0 %collective-permute-start = (bf16[1,16,1024]{2,1,0:T(8,128)(2,1)S(1)}, bf16[1,16,1024]{2,1,0:T(8,128)(2,1)S(1)}, u32[]{:S(2)}, u32[]{:S(2)}) collective-permute-start(bf16[1,16,1024]{2,1,0:T(8,128)(2,1)S(1)} %fusion.18), channel_id=1, source_target_pairs={{0,1},{1,0},{2,3},{3,2},{4,5},{5,4},{6,7},{7,6},{8,9},{9,8},{10,11... | collective-permute-start | bytes 98312 | tf_op jit(solution)/shard_map/ppermute | solution.py:25
  188.1 5.4 %collective-permute-start.1 = (bf16[2,16,1024]{2,1,0:T(8,128)(2,1)S(1)}, bf16[2,16,1024]{2,1,0:T(8,128)(2,1)S(1)}, u32[]{:S(2)}, u32[]{:S(2)}) collective-permute-start(bf16[2,16,1024]{2,1,0:T(8,128)(2,1)S(1)} %pad_maximum_fusion.2), channel_id=1, source_target_pairs={{0,2},{1,3},{2,0},{3,1},{4,6},{5,7},{6,4},{7,5},{8,10},{9,11},{10,... | collective-permute-start | bytes 196616 | tf_op jit(solution)/shard_map/ppermute | solution.py:25
  193.6 7.1 %collective-permute-start.2 = (bf16[4,16,1024]{2,1,0:T(8,128)(2,1)S(1)}, bf16[4,16,1024]{2,1,0:T(8,128)(2,1)S(1)}, u32[]{:S(2)}, u32[]{:S(2)}) collective-permute-start(bf16[4,16,1024]{2,1,0:T(8,128)(2,1)S(1)} %pad_maximum_fusion.1), channel_id=1, source_target_pairs={{0,4},{1,5},{2,6},{3,7},{4,0},{5,1},{6,2},{7,3},{8,12},{9,13},{10,... | collective-permute-start | bytes 393224 | tf_op jit(solution)/shard_map/ppermute | solution.py:25
Sparse Core Ops, SparseCore 0:
  12.9 145.2 all-reduce.1
  201.6 15.2 all-gather.1
